TPU v7x, 32 devices: a whole 2x2x4 slice. The times are simulated.
32 devices in a mesh: row: 8 (over z, core), col: 4 (over y, x).
Axes of the slice: x: 2, y: 2, z: 4, core: 2. Of those that a mesh axis runs over, the one named last changes fastest.
Arguments:
- patches: bfloat16 [8, 4, 2, 16, 128, 128], P('row', 'col'), as said below
- windows: bfloat16 [8, 4, 2, 16, 36864], P('row', 'col'), as said below
- candidates: int32 [8, 4, 2, 2, 128], P('row', 'col'), may hold values from -32 to 32, as said below
- live: int32 [8, 4, 2], replicated, may hold values from 1 to 16, as said below
- edges: int32 [8, 2, 2820], P('row', None, 'col'), may hold values from 0 to 255, as said below
- stiffness: float32 [8, 2820], P('row', 'col'), may hold values from 0.3 to 3
Outputs:
- matches: float32 [8, 4, 2, 3, 16], P('row', 'col')
- mesh_shift: float32 [8, 4, 2, 256], P('row', 'col')
Inputs may be any that keep to these rules, and one draw needn't show every extreme that they name: `candidates`: the candidate shifts of a patch need not be distinct. live[r, c, k] counts the live slots of seam k of tile (r, c): slots 0 to live - 1; the same for all devices. Each tile's springs are the edges of its 16 x 16 vertex grid, horizontal and vertical, and one diagonal of every cell, in any order. `windows`: window k of tile (r, c) serves the seam that tile (r, c-1) (k = 0) or tile (r-1, c) (k = 1) holds as its seam k. `patches`: patch p of seam k is scored against window p of the neighbour.
All inputs are finite; a program needn't handle non-finite values.
Results may differ from a plain program's by a relative error of at most 0.0003.
Values may be sent and summed in bfloat16 or wider, within the bound.
A program may use at most 64 MiB of HBM per device.

v0:
```python
import jax
import jax.numpy as jnp
from jax import lax
from jax.sharding import PartitionSpec as P

REACH = 32
WIN = 192
NS = 8
P_SIZE = 16
BLK = 4
GV = 16
ITERS = 3
LAMBDA_REG = 0.05
EPSILON = 1e-05
PRECISE = lax.Precision.HIGHEST


def shifted(x, axis, by):
    length = lax.axis_size(axis)
    pairs = [(i, i + by) for i in range(length) if 0 <= i + by < length]
    return lax.ppermute(x, axis, pairs)


def with_halo(block, sides, width):
    for axis, dim in sides:
        count = lax.axis_size(axis)
        forward = [(i, i + 1) for i in range(count - 1)]
        backward = [(target, source) for source, target in forward]
        low = lax.ppermute(
            lax.slice_in_dim(block, block.shape[dim] - width, None, axis=dim), axis, forward
        )
        high = lax.ppermute(lax.slice_in_dim(block, 0, width, axis=dim), axis, backward)
        block = jnp.concatenate([low, block, high], axis=dim)
    return block


def match_block(patch_raw, frames, list_y, list_x):
    patch_size = patch_raw.shape[-1]
    cand_count = list_y.shape[-1]
    pixel_count = float(patch_size * patch_size)
    frame_pixels_all = frames.reshape(frames.shape[0], WIN, WIN)

    def crop_all(frame_pixels, shifts_y, shifts_x):

        def crop_one(move_y, move_x):
            return lax.dynamic_slice(
                frame_pixels, (REACH + move_y, REACH + move_x), (patch_size, patch_size)
            )

        return jax.vmap(crop_one)(shifts_y, shifts_x)

    cropped = jax.vmap(crop_all)(frame_pixels_all, list_y, list_x)
    unit_plane = jnp.ones((patch_size, patch_size), patch_raw.dtype)
    patch_sum = jnp.einsum("byx,yx->b", patch_raw, unit_plane, preferred_element_type=jnp.float32)
    patch_square = jnp.einsum(
        "byx,byx->b", patch_raw, patch_raw, preferred_element_type=jnp.float32
    )
    crop_sum = jnp.einsum("bsyx,yx->bs", cropped, unit_plane, preferred_element_type=jnp.float32)
    crop_square = jnp.einsum("bsyx,bsyx->bs", cropped, cropped, preferred_element_type=jnp.float32)
    cross_sum = jnp.einsum("byx,bsyx->bs", patch_raw, cropped, preferred_element_type=jnp.float32)
    patch_mean = patch_sum / pixel_count
    crop_mean = crop_sum / pixel_count
    patch_var = patch_square / pixel_count - patch_mean * patch_mean
    crop_var = crop_square / pixel_count - crop_mean * crop_mean
    cross_mean = cross_sum / pixel_count - patch_mean[:, None] * crop_mean
    correl = cross_mean / jnp.sqrt((patch_var[:, None] + EPSILON) * (crop_var + EPSILON))
    weight = (1.5 + correl) * (1.5 + correl)
    weight_sum = jnp.sum(weight, axis=1)
    along_y = jnp.sum(weight * list_y.astype(jnp.float32), axis=1) / (REACH * weight_sum)
    along_x = jnp.sum(weight * list_x.astype(jnp.float32), axis=1) / (REACH * weight_sum)
    return jnp.stack([along_y, along_x, weight_sum / cand_count])


def match_strip(patch_raw, frames, shift_list, live_count):
    shifts = shift_list.reshape(2, P_SIZE, NS)
    blocks = (live_count + BLK - 1) // BLK

    def one_block(block_index, result):
        block_start = (block_index * BLK).astype(jnp.int32)
        scored = match_block(
            lax.dynamic_slice_in_dim(patch_raw, block_start, BLK, 0),
            lax.dynamic_slice_in_dim(frames, block_start, BLK, 0),
            lax.dynamic_slice_in_dim(shifts[0], block_start, BLK, 0),
            lax.dynamic_slice_in_dim(shifts[1], block_start, BLK, 0),
        )
        return lax.dynamic_update_slice(result, scored, (jnp.zeros((), jnp.int32), block_start))

    result = lax.fori_loop(0, blocks, one_block, jnp.zeros((3, P_SIZE), jnp.float32))
    keeper = (jnp.arange(P_SIZE) < live_count).astype(jnp.float32)
    return result * keeper


def body(patches, windows, candidates, live, edges, stiffness):
    tile_row = lax.axis_index("row")
    tile_col = lax.axis_index("col")
    last_row = lax.axis_size("row") - 1
    last_col = lax.axis_size("col") - 1
    far_east = shifted(windows[0, 0, 0], "col", -1)
    far_south = shifted(windows[0, 0, 1], "row", -1)
    count_east = jnp.where(tile_col < last_col, live[tile_row, tile_col, 0], 0)
    count_south = jnp.where(tile_row < last_row, live[tile_row, tile_col, 1], 0)
    own_east = match_strip(patches[0, 0, 0], far_east, candidates[0, 0, 0], count_east)
    own_south = match_strip(patches[0, 0, 1], far_south, candidates[0, 0, 1], count_south)
    from_west = shifted(own_east, "col", 1)
    from_north = shifted(own_south, "row", 1)
    matches = jnp.stack([own_east, own_south])[None, None]
    slots = jnp.arange(P_SIZE)
    picker = (jnp.arange(GV)[None, :] == (slots * GV // P_SIZE)[:, None]).astype(jnp.float32)
    vertex = jnp.arange(GV * GV)
    incidence = (edges[0, 0][:, None] == vertex[None, :]).astype(jnp.float32) - (
        edges[0, 1][:, None] == vertex[None, :]
    ).astype(jnp.float32)
    spring = stiffness[0]

    def spread(values):
        return jnp.dot(values, picker, precision=PRECISE)

    def sample(values):
        return jnp.dot(values, picker.T, precision=PRECISE)

    conf_east = own_east[2]
    conf_south = own_south[2]
    conf_west = from_west[2]
    conf_north = from_north[2]

    def operate(vector):
        border = with_halo(vector, (("row", 1), ("col", 2)), 1)
        flat_field = vector.reshape(2, GV * GV)
        stretch = jnp.dot(flat_field, incidence.T, precision=PRECISE) * spring
        output = (LAMBDA_REG * flat_field + jnp.dot(stretch, incidence, precision=PRECISE)).reshape(
            2, GV, GV
        )
        output = output.at[:, :, GV - 1].add(
            spread(conf_east * sample(vector[:, :, GV - 1] - border[:, 1:-1, -1]))
        )
        output = output.at[:, :, 0].add(
            spread(conf_west * sample(vector[:, :, 0] - border[:, 1:-1, 0]))
        )
        output = output.at[:, GV - 1, :].add(
            spread(conf_south * sample(vector[:, GV - 1, :] - border[:, -1, 1:-1]))
        )
        output = output.at[:, 0, :].add(
            spread(conf_north * sample(vector[:, 0, :] - border[:, 0, 1:-1]))
        )
        return output

    forcing = jnp.zeros((2, GV, GV), jnp.float32)
    forcing = forcing.at[:, :, GV - 1].add(spread(conf_east * own_east[:2]))
    forcing = forcing.at[:, :, 0].add(-spread(conf_west * from_west[:2]))
    forcing = forcing.at[:, GV - 1, :].add(spread(conf_south * own_south[:2]))
    forcing = forcing.at[:, 0, :].add(-spread(conf_north * from_north[:2]))
    solution = jnp.zeros_like(forcing)
    residual = forcing

    def two_products(values, applied):
        return lax.psum((jnp.sum(values * values), jnp.sum(values * applied)), ("row", "col"))

    applied = operate(residual)
    norm_now, product = two_products(residual, applied)
    step_length = norm_now / product
    direction = residual
    along = applied
    for iteration in range(ITERS):
        solution = solution + step_length * direction
        residual = residual - step_length * along
        if iteration + 1 < ITERS:
            applied = operate(residual)
            norm_next, product = two_products(residual, applied)
            beta_ratio = norm_next / norm_now
            step_length = norm_next / (product - beta_ratio * norm_next / step_length)
            direction = residual + beta_ratio * direction
            along = applied + beta_ratio * along
            norm_now = norm_next
    mesh_shift = solution.reshape(2, GV * GV)[None, None]
    return (matches, mesh_shift)


def solution(mesh):
    return jax.shard_map(
        body,
        mesh=mesh,
        in_specs=(
            P("row", "col", None, None, None, None),
            P("row", "col", None, None, None),
            P("row", "col", None, None, None),
            P(),
            P("row", None, "col"),
            P("row", "col"),
        ),
        out_specs=(P("row", "col", None, None, None), P("row", "col", None, None)),
        check_vma=False,
    )
```

profile of v0, /device:TPU:0, one launch (start us, length us, event | category | flops | bytes accessed | tf_op | source)
XLA Modules:
  0.0 767.8 jit_solution(11452853252674101553)
XLA Ops:
  0.7 2.9 slice_bitcast_fusion.1
  12.0 91.7 %while.49 = (s32[]{:T(128)}, f32[3,16]{1,0:T(4,128)S(1)}, s32[]{:T(128)}, bf16[16,128,128]{2,1,0:T(8,128)(2,1)S(1)}, bf16[16,36864]{1,0:T(8,128)(2,1)}, /*index=...) while((s32[]{:T(128)}, f32[3,16]{1,0:T(4,128)S(1)}, ...), condition=%wide.region_9.10_spmd, body=%wide.region_5.9_spmd.sunk | while | flops 5178357 | bytes 5322758 | solution.py:88
  14.3 87.7 %while.51 = (s32[]{:T(128)}, bf16[4,192,192]{2,1,0:T(8,128)(2,1)S(1)}, s32[32,3]{0,1:T(4,128)S(1)}, bf16[32,128,128]{2,1,0:T(8,128)(2,1)S(1)}, s32[]{:T(128)}) while((s32[]{:T(128)}, bf16[4,192,192]{2,1,0:T(8,128)(2,1)S(1)}, s32[32,3]{0,1:T(4,128)S(1)}, bf16[32,128,128]{2,1,0:T(8,128)(2,1)S(1)}, s32[]{:T(128)}) %tuple.207), condition=%wide.while_cond.17, body=%wide.while_body.17.sunk | while | flops 2 | bytes 65665 | solution.py:46
  15.0 2.0 dynamic-slice_dynamic-update-slice_fusion.4
  17.7 2.0 dynamic-slice_dynamic-update-slice_fusion.4
  20.4 2.0 dynamic-slice_dynamic-update-slice_fusion.4
  23.2 2.0 dynamic-slice_dynamic-update-slice_fusion.4
  25.9 2.0 dynamic-slice_dynamic-update-slice_fusion.4
  28.7 2.0 dynamic-slice_dynamic-update-slice_fusion.4
  31.4 2.0 dynamic-slice_dynamic-update-slice_fusion.4
  34.1 2.0 dynamic-slice_dynamic-update-slice_fusion.4
  36.9 2.0 dynamic-slice_dynamic-update-slice_fusion.4
  39.6 2.0 dynamic-slice_dynamic-update-slice_fusion.4
  42.4 2.0 dynamic-slice_dynamic-update-slice_fusion.4
  45.1 2.0 dynamic-slice_dynamic-update-slice_fusion.4
  47.8 2.0 dynamic-slice_dynamic-update-slice_fusion.4
  50.6 2.0 dynamic-slice_dynamic-update-slice_fusion.4
  53.3 2.0 dynamic-slice_dynamic-update-slice_fusion.4
  56.1 2.0 dynamic-slice_dynamic-update-slice_fusion.4
  58.8 2.0 dynamic-slice_dynamic-update-slice_fusion.4
  61.5 2.0 dynamic-slice_dynamic-update-slice_fusion.4
  64.3 2.0 dynamic-slice_dynamic-update-slice_fusion.4
  67.0 2.0 dynamic-slice_dynamic-update-slice_fusion.4
  69.8 2.0 dynamic-slice_dynamic-update-slice_fusion.4
  72.5 2.0 dynamic-slice_dynamic-update-slice_fusion.4
  75.2 2.0 dynamic-slice_dynamic-update-slice_fusion.4
  78.0 2.0 dynamic-slice_dynamic-update-slice_fusion.4
  80.7 2.0 dynamic-slice_dynamic-update-slice_fusion.4
  83.5 2.0 dynamic-slice_dynamic-update-slice_fusion.4
  86.2 2.0 dynamic-slice_dynamic-update-slice_fusion.4
  88.9 2.0 dynamic-slice_dynamic-update-slice_fusion.4
  91.7 2.0 dynamic-slice_dynamic-update-slice_fusion.4
  94.4 2.0 dynamic-slice_dynamic-update-slice_fusion.4
  97.1 2.0 dynamic-slice_dynamic-update-slice_fusion.4
  99.9 2.0 dynamic-slice_dynamic-update-slice_fusion.4
  103.7 12.8 %collective-permute-start.3 = (f32[3,16]{1,0:T(4,128)S(1)}, f32[3,16]{1,0:T(4,128)S(1)}, u32[]{:S(2)}, u32[]{:S(2)}) collective-permute-start(f32[3,16]{1,0:T(4,128)S(1)} %broadcast_multiply_fusion.2), channel_id=1, source_target_pairs={{0,4},{4,8},{8,12},{12,16},{16,20},{20,24},{24,28},{1,5},{5,9},{9,... | collective-permute-start | bytes 584 | tf_op jit(solution)/shard_map/ppermute | solution.py:21
  116.6 88.6 %while.47 = (s32[]{:T(128)}, f32[3,16]{1,0:T(4,128)S(1)}, s32[]{:T(128)}, bf16[16,128,128]{2,1,0:T(8,128)(2,1)S(1)}, bf16[16,36864]{1,0:T(8,128)(2,1)}, /*index=...) while((s32[]{:T(128)}, f32[3,16]{1,0:T(4,128)S(1)}, ...), condition=%wide.region_4.5_spmd, body=%wide.region_0.4_spmd.sunk | while | flops 5178357 | bytes 5314510 | solution.py:88
  118.5 85.1 %while.50 = (s32[]{:T(128)}, bf16[4,192,192]{2,1,0:T(8,128)(2,1)S(1)}, s32[32,3]{0,1:T(4,128)S(1)}, bf16[32,128,128]{2,1,0:T(8,128)(2,1)S(1)}, s32[]{:T(128)}) while((s32[]{:T(128)}, bf16[4,192,192]{2,1,0:T(8,128)(2,1)S(1)}, s32[32,3]{0,1:T(4,128)S(1)}, bf16[32,128,128]{2,1,0:T(8,128)(2,1)S(1)}, s32[]{:T(128)}) %tuple.210), condition=%wide.while_cond.16, body=%wide.while_body.16.sunk | while | flops 2 | bytes 65665 | solution.py:46
  205.3 183.9 %collective-permute-start.2 = (f32[3,16]{1,0:T(4,128)S(1)}, f32[3,16]{1,0:T(4,128)S(1)}, u32[]{:S(2)}, u32[]{:S(2)}) collective-permute-start(f32[3,16]{1,0:T(4,128)S(1)} %broadcast_multiply_fusion.3), channel_id=1, source_target_pairs={{0,1},{1,2},{2,3},{4,5},{5,6},{6,7},{8,9},{9,10},{10,11},{12,13},{... | collective-permute-start | bytes 584 | tf_op jit(solution)/shard_map/ppermute | solution.py:21
  395.5 3.4 collective-permute-start.4
  401.7 184.5 %collective-permute-start.7 = (f32[2,18,1]{1,0,2:T(2,128)S(1)}, f32[2,18,1]{1,0,2:T(2,128)S(1)}, u32[]{:S(2)}, u32[]{:S(2)}) collective-permute-start(f32[2,18,1]{1,0,2:T(2,128)S(1)} %get-tuple-element.508), channel_id=1, source_target_pairs={{0,1},{1,2},{2,3},{4,5},{5,6},{6,7},{8,9},{9,10},{10,11},{12,13},{... | collective-permute-start | bytes 440 | tf_op jit(solution)/shard_map/ppermute | solution.py:29
  590.0 43.7 %all-reduce.3 = (f32[]{:T(128)}, f32[]{:T(128)}) all-reduce(f32[]{:T(128)} %get-tuple-element.427, f32[]{:T(128)} %get-tuple-element.426), channel_id=1, replica_groups=mesh['row'=8,'col'=4] {'row','col'}, use_global_device_ids=true, to_apply=%region_11.12 | all-reduce | flops 2 | bytes 16 | tf_op jit(solution)/shard_map/psum | solution.py:156
  640.1 3.5 collective-permute-done.9
  645.7 4.8 collective-permute-start.11
  654.6 43.1 %all-reduce.2 = (f32[]{:T(128)}, f32[]{:T(128)}) all-reduce(f32[]{:T(128)} %get-tuple-element.425, f32[]{:T(128)} %get-tuple-element.424), channel_id=1, replica_groups=mesh['row'=8,'col'=4] {'row','col'}, use_global_device_ids=true, to_apply=%region_15.16 | all-reduce | flops 2 | bytes 16 | tf_op jit(solution)/shard_map/psum | solution.py:156
  707.2 2.2 collective-permute-done.13
  711.5 4.8 collective-permute-start.15
  720.1 43.0 %all-reduce.1 = (f32[]{:T(128)}, f32[]{:T(128)}) all-reduce(f32[]{:T(128)} %get-tuple-element.423, f32[]{:T(128)} %get-tuple-element.422), channel_id=1, replica_groups=mesh['row'=8,'col'=4] {'row','col'}, use_global_device_ids=true, to_apply=%region_19.20 | all-reduce | flops 2 | bytes 16 | tf_op jit(solution)/shard_map/psum | solution.py:156
  (364 shorter events, 156.0 us)
Async XLA Ops:
  0.6 8.2 %copy-start.10 = (s32[1,1,2,2,128]{4,3,2,1,0:T(2,128)S(1)}, s32[1,1,2,2,128]{4,3,2,1,0:T(2,128)}, u32[]{:S(2)}) copy-start(s32[1,1,2,2,128]{4,3,2,1,0:T(2,128)} %param.44) | copy-start | bytes 6148
  0.6 8.4 %copy-start.7 = (f32[1,705]{1,0:T(1,128)S(1)}, f32[1,705]{1,0:T(1,128)}, u32[]{:S(2)}) copy-start(f32[1,705]{1,0:T(1,128)} %param.47) | copy-start | bytes 8464
  0.7 10.6 %copy-start.3 = (s32[1,2,705]{2,1,0:T(2,128)S(1)}, s32[1,2,705]{2,1,0:T(2,128)}, u32[]{:S(2)}) copy-start(s32[1,2,705]{2,1,0:T(2,128)} %param.46) | copy-start | bytes 16924
  0.7 11.2 %copy-start = (bf16[1,1,2,16,128,128]{5,4,3,2,1,0:T(8,128)(2,1)S(1)}, bf16[1,1,2,16,128,128]{5,4,3,2,1,0:T(8,128)(2,1)}, u32[]{:S(2)}) copy-start(bf16[1,1,2,16,128,128]{5,4,3,2,1,0:T(8,128)(2,1)} %param.42) | copy-start | bytes 3145732
  3.6 8.4 %collective-permute-start.1 = (bf16[16,36864]{1,0:T(8,128)(2,1)S(1)}, bf16[16,36864]{1,0:T(8,128)(2,1)}, u32[]{:S(2)}, u32[]{:S(2)}) collective-permute-start(bf16[16,36864]{1,0:T(8,128)(2,1)S(1)} %get-tuple-element.501), channel_id=1, source_target_pairs={{4,0},{8,4},{12,8},{16,12},{20,16},{24,20},{28,24},{5,1},{9,5},{13... | collective-permute-start | bytes 3538952 | tf_op jit(solution)/shard_map/ppermute | solution.py:21
  4.9 111.7 %collective-permute-start = (bf16[16,36864]{1,0:T(8,128)(2,1)}, bf16[16,36864]{1,0:T(8,128)(2,1)}, u32[]{:S(2)}, u32[]{:S(2)}) collective-permute-start(bf16[16,36864]{1,0:T(8,128)(2,1)} %get-tuple-element.500), channel_id=1, source_target_pairs={{1,0},{2,1},{3,2},{5,4},{6,5},{7,6},{9,8},{10,9},{11,10},{13,12},{... | collective-permute-start | bytes 3538952 | tf_op jit(solution)/shard_map/ppermute | solution.py:21
  12.0 91.7 %copy-start.8 = (f32[16]{0:T(128)S(1)}, f32[16]{0:T(128)}, u32[]{:S(2)}) copy-start(f32[16]{0:T(128)} %compare_convert_fusion) | copy-start | bytes 196
  12.0 0.6 copy-start.1
  101.9 1.7 copy-start.2
  103.7 286.6 %collective-permute-start.3 = (f32[3,16]{1,0:T(4,128)S(1)}, f32[3,16]{1,0:T(4,128)S(1)}, u32[]{:S(2)}, u32[]{:S(2)}) collective-permute-start(f32[3,16]{1,0:T(4,128)S(1)} %broadcast_multiply_fusion.2), channel_id=1, source_target_pairs={{0,4},{4,8},{8,12},{12,16},{16,20},{20,24},{24,28},{1,5},{5,9},{9,... | collective-permute-start | bytes 584 | tf_op jit(solution)/shard_map/ppermute | solution.py:21
  116.6 88.7 %copy-start.9 = (f32[16]{0:T(128)S(1)}, f32[16]{0:T(128)}, u32[]{:S(2)}) copy-start(f32[16]{0:T(128)} %compare_convert_fusion.1) | copy-start | bytes 196
  116.6 272.6 %copy-start.11 = (s32[16]{0:T(128)S(1)}, s32[16]{0:T(128)}, u32[]{:S(2)}) copy-start(s32[16]{0:T(128)} %and_select_fusion) | copy-start | bytes 196
  116.6 277.2 %copy-start.4 = (s32[705]{0:T(1024)S(1)}, s32[705]{0:T(1024)}, u32[]{:S(2)}) copy-start(s32[705]{0:T(1024)} %get-tuple-element.428) | copy-start | bytes 8464
  116.6 277.1 %copy-start.5 = (s32[705]{0:T(1024)S(1)}, s32[705]{0:T(1024)}, u32[]{:S(2)}) copy-start(s32[705]{0:T(1024)} %get-tuple-element.429) | copy-start | bytes 8464
  116.6 277.1 %copy-start.6 = (f32[705]{0:T(1024)S(1)}, f32[705]{0:T(1024)}, u32[]{:S(2)}) copy-start(f32[705]{0:T(1024)} %reduce.44) | copy-start | bytes 8464
  205.3 185.3 %collective-permute-start.2 = (f32[3,16]{1,0:T(4,128)S(1)}, f32[3,16]{1,0:T(4,128)S(1)}, u32[]{:S(2)}, u32[]{:S(2)}) collective-permute-start(f32[3,16]{1,0:T(4,128)S(1)} %broadcast_multiply_fusion.3), channel_id=1, source_target_pairs={{0,1},{1,2},{2,3},{4,5},{5,6},{6,7},{8,9},{9,10},{10,11},{12,13},{... | collective-permute-start | bytes 584 | tf_op jit(solution)/shard_map/ppermute | solution.py:21
  392.1 3.3 collective-permute-start.5
  395.5 4.2 collective-permute-start.4
  400.4 185.8 %collective-permute-start.6 = (f32[2,18,1]{1,0,2:T(2,128)S(1)}, f32[2,18,1]{1,0,2:T(2,128)S(1)}, u32[]{:S(2)}, u32[]{:S(2)}) collective-permute-start(f32[2,18,1]{1,0,2:T(2,128)S(1)} %get-tuple-element.509), channel_id=1, source_target_pairs={{1,0},{2,1},{3,2},{5,4},{6,5},{7,6},{9,8},{10,9},{11,10},{13,12},{... | collective-permute-start | bytes 440 | tf_op jit(solution)/shard_map/ppermute | solution.py:32
  401.7 185.8 %collective-permute-start.7 = (f32[2,18,1]{1,0,2:T(2,128)S(1)}, f32[2,18,1]{1,0,2:T(2,128)S(1)}, u32[]{:S(2)}, u32[]{:S(2)}) collective-permute-start(f32[2,18,1]{1,0,2:T(2,128)S(1)} %get-tuple-element.508), channel_id=1, source_target_pairs={{0,1},{1,2},{2,3},{4,5},{5,6},{6,7},{8,9},{9,10},{10,11},{12,13},{... | collective-permute-start | bytes 440 | tf_op jit(solution)/shard_map/ppermute | solution.py:29
  635.2 3.0 collective-permute-start.8
  638.5 5.1 collective-permute-start.9
  644.4 6.1 collective-permute-start.10
  645.7 6.1 collective-permute-start.11
  702.2 3.0 collective-permute-start.12
  705.6 3.8 collective-permute-start.13
  710.2 6.1 collective-permute-start.14
  711.5 6.1 collective-permute-start.15
where the time goes:
time: 774 us; the launch traced here: 768 us
  starting transfers between devices  407 us (53%)
  local copies, waits for them, and re-layouts  191 us (25%)
  blocking collectives  130 us (17%)
  between operations  12.4 us (2%)
  matrix products  9.82 us (1%)
  waiting for transfers between devices  8.69 us (1%)
  other arithmetic  8.31 us (1%)
    ppermute x6, starting transfers between devices, with_halo(): lax.ppermute(lax.slice_in_dim(block, block.shape[dim] - width, None, axis...  200 us
    ppermute x4, starting transfers between devices, shifted(): return lax.ppermute(x, axis, pairs)  199 us
    gather x192, local copies, waits for them, and re-layouts  172 us
    psum x3, blocking collectives, two_products(): lax.psum((jnp.sum(values * values), jnp.sum(values * applied)), ('row', '...  130 us
  transfers between devices with their start and end apart: 16, of which 6 were waited for; matrix products, arithmetic and copies ran while one was open for 25% of the time, Pallas kernels for 0%

commit v1 on v0

--- a/solution.py
+++ b/solution.py
@@ -153,7 +153,9 @@
     residual = forcing
 
     def two_products(values, applied):
-        return lax.psum((jnp.sum(values * values), jnp.sum(values * applied)), ("row", "col"))
+        return lax.psum(
+            lax.psum((jnp.sum(values * values), jnp.sum(values * applied)), "col"), "row"
+        )
 
     applied = operate(residual)
     norm_now, product = two_products(residual, applied)

time: 774 us -> 720 us (0.930)
  blocking collectives: 130 us -> 77.9 us
    psum x3 -> x6, blocking collectives: 130 us -> 77.9 us  [the longest x3 43.2 us: two_products(): lax.psum(lax.psum((jnp.sum(values * values), jnp.sum(values * applied)),...]
  transfers between devices with their start and end apart: 16 -> 16, of which waited for: 6 -> 6; matrix products, arithmetic and copies ran while one was open for 25% -> 27% of each run, Pallas kernels for 0% -> 0%
where the time goes in v1:
time: 720 us; the launch traced here: 714 us
  starting transfers between devices  408 us (57%)
  local copies, waits for them, and re-layouts  190 us (26%)
  blocking collectives  77.9 us (11%)
  between operations  12.2 us (2%)
  matrix products  9.82 us (1%)
  other arithmetic  8.37 us (1%)
    ppermute x6, starting transfers between devices, with_halo(): lax.ppermute(lax.slice_in_dim(block, block.shape[dim] - width, None, axis...  201 us
    ppermute x4, starting transfers between devices, shifted(): return lax.ppermute(x, axis, pairs)  199 us
    gather x192, local copies, waits for them, and re-layouts  172 us
    psum x3, blocking collectives, two_products(): lax.psum(lax.psum((jnp.sum(values * values), jnp.sum(values * applied)),...  43.2 us
    psum x3, blocking collectives, two_products(): lax.psum((jnp.sum(values * values), jnp.sum(values * applied)), 'col')  34.7 us
  transfers between devices with their start and end apart: 16, of which 6 were waited for; matrix products, arithmetic and copies ran while one was open for 27% of the time, Pallas kernels for 0%

profile of v1, /device:TPU:0, one launch (start us, length us, event | category | flops | bytes accessed | tf_op | source)
XLA Modules:
  0.0 714.0 jit_solution(211408834463326193)
XLA Ops:
  0.7 2.9 slice_bitcast_fusion.1
  12.0 91.7 %while.49 = (s32[]{:T(128)}, f32[3,16]{1,0:T(4,128)S(1)}, s32[]{:T(128)}, bf16[16,128,128]{2,1,0:T(8,128)(2,1)S(1)}, bf16[16,36864]{1,0:T(8,128)(2,1)}, /*index=...) while((s32[]{:T(128)}, f32[3,16]{1,0:T(4,128)S(1)}, ...), condition=%wide.region_9.10_spmd, body=%wide.region_5.9_spmd.sunk | while | flops 5178357 | bytes 5322758 | solution.py:88
  14.3 87.7 %while.51 = (s32[]{:T(128)}, bf16[4,192,192]{2,1,0:T(8,128)(2,1)S(1)}, s32[32,3]{0,1:T(4,128)S(1)}, bf16[32,128,128]{2,1,0:T(8,128)(2,1)S(1)}, s32[]{:T(128)}) while((s32[]{:T(128)}, bf16[4,192,192]{2,1,0:T(8,128)(2,1)S(1)}, s32[32,3]{0,1:T(4,128)S(1)}, bf16[32,128,128]{2,1,0:T(8,128)(2,1)S(1)}, s32[]{:T(128)}) %tuple.207), condition=%wide.while_cond.17, body=%wide.while_body.17.sunk | while | flops 2 | bytes 65665 | solution.py:46
  15.0 2.0 dynamic-slice_dynamic-update-slice_fusion.4
  17.7 2.0 dynamic-slice_dynamic-update-slice_fusion.4
  20.4 2.0 dynamic-slice_dynamic-update-slice_fusion.4
  23.2 2.0 dynamic-slice_dynamic-update-slice_fusion.4
  25.9 2.0 dynamic-slice_dynamic-update-slice_fusion.4
  28.7 2.0 dynamic-slice_dynamic-update-slice_fusion.4
  31.4 2.0 dynamic-slice_dynamic-update-slice_fusion.4
  34.1 2.0 dynamic-slice_dynamic-update-slice_fusion.4
  36.9 2.0 dynamic-slice_dynamic-update-slice_fusion.4
  39.6 2.0 dynamic-slice_dynamic-update-slice_fusion.4
  42.4 2.0 dynamic-slice_dynamic-update-slice_fusion.4
  45.1 2.0 dynamic-slice_dynamic-update-slice_fusion.4
  47.8 2.0 dynamic-slice_dynamic-update-slice_fusion.4
  50.6 2.0 dynamic-slice_dynamic-update-slice_fusion.4
  53.3 2.0 dynamic-slice_dynamic-update-slice_fusion.4
  56.1 2.0 dynamic-slice_dynamic-update-slice_fusion.4
  58.8 2.0 dynamic-slice_dynamic-update-slice_fusion.4
  61.5 2.0 dynamic-slice_dynamic-update-slice_fusion.4
  64.3 2.0 dynamic-slice_dynamic-update-slice_fusion.4
  67.0 2.0 dynamic-slice_dynamic-update-slice_fusion.4
  69.8 2.0 dynamic-slice_dynamic-update-slice_fusion.4
  72.5 2.0 dynamic-slice_dynamic-update-slice_fusion.4
  75.2 2.0 dynamic-slice_dynamic-update-slice_fusion.4
  80.7 2.0 dynamic-slice_dynamic-update-slice_fusion.4
  83.5 2.0 dynamic-slice_dynamic-update-slice_fusion.4
  88.9 2.0 dynamic-slice_dynamic-update-slice_fusion.4
  91.7 2.0 dynamic-slice_dynamic-update-slice_fusion.4
  94.4 2.0 dynamic-slice_dynamic-update-slice_fusion.4
  97.1 2.0 dynamic-slice_dynamic-update-slice_fusion.4
  99.9 2.0 dynamic-slice_dynamic-update-slice_fusion.4
  103.7 12.8 %collective-permute-start.3 = (f32[3,16]{1,0:T(4,128)S(1)}, f32[3,16]{1,0:T(4,128)S(1)}, u32[]{:S(2)}, u32[]{:S(2)}) collective-permute-start(f32[3,16]{1,0:T(4,128)S(1)} %broadcast_multiply_fusion.2), channel_id=1, source_target_pairs={{0,4},{4,8},{8,12},{12,16},{16,20},{20,24},{24,28},{1,5},{5,9},{9,... | collective-permute-start | bytes 584 | tf_op jit(solution)/shard_map/ppermute | solution.py:21
  116.6 88.6 %while.47 = (s32[]{:T(128)}, f32[3,16]{1,0:T(4,128)S(1)}, s32[]{:T(128)}, bf16[16,128,128]{2,1,0:T(8,128)(2,1)S(1)}, bf16[16,36864]{1,0:T(8,128)(2,1)}, /*index=...) while((s32[]{:T(128)}, f32[3,16]{1,0:T(4,128)S(1)}, ...), condition=%wide.region_4.5_spmd, body=%wide.region_0.4_spmd.sunk | while | flops 5178357 | bytes 5314510 | solution.py:88
  118.5 85.1 %while.50 = (s32[]{:T(128)}, bf16[4,192,192]{2,1,0:T(8,128)(2,1)S(1)}, s32[32,3]{0,1:T(4,128)S(1)}, bf16[32,128,128]{2,1,0:T(8,128)(2,1)S(1)}, s32[]{:T(128)}) while((s32[]{:T(128)}, bf16[4,192,192]{2,1,0:T(8,128)(2,1)S(1)}, s32[32,3]{0,1:T(4,128)S(1)}, bf16[32,128,128]{2,1,0:T(8,128)(2,1)S(1)}, s32[]{:T(128)}) %tuple.210), condition=%wide.while_cond.16, body=%wide.while_body.16.sunk | while | flops 2 | bytes 65665 | solution.py:46
  205.3 183.9 %collective-permute-start.2 = (f32[3,16]{1,0:T(4,128)S(1)}, f32[3,16]{1,0:T(4,128)S(1)}, u32[]{:S(2)}, u32[]{:S(2)}) collective-permute-start(f32[3,16]{1,0:T(4,128)S(1)} %broadcast_multiply_fusion.3), channel_id=1, source_target_pairs={{0,1},{1,2},{2,3},{4,5},{5,6},{6,7},{8,9},{9,10},{10,11},{12,13},{... | collective-permute-start | bytes 584 | tf_op jit(solution)/shard_map/ppermute | solution.py:21
  395.5 3.4 collective-permute-start.4
  401.7 184.5 %collective-permute-start.7 = (f32[2,18,1]{1,0,2:T(2,128)S(1)}, f32[2,18,1]{1,0,2:T(2,128)S(1)}, u32[]{:S(2)}, u32[]{:S(2)}) collective-permute-start(f32[2,18,1]{1,0,2:T(2,128)S(1)} %get-tuple-element.514), channel_id=1, source_target_pairs={{0,1},{1,2},{2,3},{4,5},{5,6},{6,7},{8,9},{9,10},{10,11},{12,13},{... | collective-permute-start | bytes 440 | tf_op jit(solution)/shard_map/ppermute | solution.py:29
  590.1 13.0 %all-reduce.6 = (f32[]{:T(128)}, f32[]{:T(128)}) all-reduce(f32[]{:T(128)} %get-tuple-element.427, f32[]{:T(128)} %get-tuple-element.426), channel_id=1, replica_groups=mesh['row'=8,'col'=4] {'col'}, use_global_device_ids=true, to_apply=%region_11.12 | all-reduce | flops 2 | bytes 16 | tf_op jit(solution)/shard_map/psum | solution.py:157
  603.1 14.7 %all-reduce.3 = (f32[]{:T(128)}, f32[]{:T(128)}) all-reduce(f32[]{:T(128)} %get-tuple-element.480, f32[]{:T(128)} %get-tuple-element.481), channel_id=1, replica_groups=mesh['row'=8,'col'=4] {'row'}, use_global_device_ids=true, to_apply=%region_12.13 | all-reduce | flops 2 | bytes 16 | tf_op jit(solution)/shard_map/psum | solution.py:156
  619.3 2.2 collective-permute-start.8
  628.8 4.5 collective-permute-start.11
  637.2 10.4 %all-reduce.5 = (f32[]{:T(128)}, f32[]{:T(128)}) all-reduce(f32[]{:T(128)} %get-tuple-element.425, f32[]{:T(128)} %get-tuple-element.424), channel_id=1, replica_groups=mesh['row'=8,'col'=4] {'col'}, use_global_device_ids=true, to_apply=%region_17.18 | all-reduce | flops 2 | bytes 16 | tf_op jit(solution)/shard_map/psum | solution.py:157
  647.6 14.2 %all-reduce.2 = (f32[]{:T(128)}, f32[]{:T(128)}) all-reduce(f32[]{:T(128)} %get-tuple-element.478, f32[]{:T(128)} %get-tuple-element.479), channel_id=1, replica_groups=mesh['row'=8,'col'=4] {'row'}, use_global_device_ids=true, to_apply=%region_18.19 | all-reduce | flops 2 | bytes 16 | tf_op jit(solution)/shard_map/psum | solution.py:156
  675.5 4.5 collective-permute-start.15
  683.9 11.3 %all-reduce.4 = (f32[]{:T(128)}, f32[]{:T(128)}) all-reduce(f32[]{:T(128)} %get-tuple-element.423, f32[]{:T(128)} %get-tuple-element.422), channel_id=1, replica_groups=mesh['row'=8,'col'=4] {'col'}, use_global_device_ids=true, to_apply=%region_23.24 | all-reduce | flops 2 | bytes 16 | tf_op jit(solution)/shard_map/psum | solution.py:157
  695.2 14.2 %all-reduce.1 = (f32[]{:T(128)}, f32[]{:T(128)}) all-reduce(f32[]{:T(128)} %get-tuple-element.476, f32[]{:T(128)} %get-tuple-element.477), channel_id=1, replica_groups=mesh['row'=8,'col'=4] {'row'}, use_global_device_ids=true, to_apply=%region_24.25 | all-reduce | flops 2 | bytes 16 | tf_op jit(solution)/shard_map/psum | solution.py:156
  (367 shorter events, 162.4 us)
Async XLA Ops:
  0.6 8.2 %copy-start.10 = (s32[1,1,2,2,128]{4,3,2,1,0:T(2,128)S(1)}, s32[1,1,2,2,128]{4,3,2,1,0:T(2,128)}, u32[]{:S(2)}) copy-start(s32[1,1,2,2,128]{4,3,2,1,0:T(2,128)} %param.44) | copy-start | bytes 6148
  0.6 8.4 %copy-start.7 = (f32[1,705]{1,0:T(1,128)S(1)}, f32[1,705]{1,0:T(1,128)}, u32[]{:S(2)}) copy-start(f32[1,705]{1,0:T(1,128)} %param.47) | copy-start | bytes 8464
  0.7 10.6 %copy-start.3 = (s32[1,2,705]{2,1,0:T(2,128)S(1)}, s32[1,2,705]{2,1,0:T(2,128)}, u32[]{:S(2)}) copy-start(s32[1,2,705]{2,1,0:T(2,128)} %param.46) | copy-start | bytes 16924
  0.7 11.2 %copy-start = (bf16[1,1,2,16,128,128]{5,4,3,2,1,0:T(8,128)(2,1)S(1)}, bf16[1,1,2,16,128,128]{5,4,3,2,1,0:T(8,128)(2,1)}, u32[]{:S(2)}) copy-start(bf16[1,1,2,16,128,128]{5,4,3,2,1,0:T(8,128)(2,1)} %param.42) | copy-start | bytes 3145732
  3.6 8.4 %collective-permute-start.1 = (bf16[16,36864]{1,0:T(8,128)(2,1)S(1)}, bf16[16,36864]{1,0:T(8,128)(2,1)}, u32[]{:S(2)}, u32[]{:S(2)}) collective-permute-start(bf16[16,36864]{1,0:T(8,128)(2,1)S(1)} %get-tuple-element.507), channel_id=1, source_target_pairs={{4,0},{8,4},{12,8},{16,12},{20,16},{24,20},{28,24},{5,1},{9,5},{13... | collective-permute-start | bytes 3538952 | tf_op jit(solution)/shard_map/ppermute | solution.py:21
  4.9 111.7 %collective-permute-start = (bf16[16,36864]{1,0:T(8,128)(2,1)}, bf16[16,36864]{1,0:T(8,128)(2,1)}, u32[]{:S(2)}, u32[]{:S(2)}) collective-permute-start(bf16[16,36864]{1,0:T(8,128)(2,1)} %get-tuple-element.506), channel_id=1, source_target_pairs={{1,0},{2,1},{3,2},{5,4},{6,5},{7,6},{9,8},{10,9},{11,10},{13,12},{... | collective-permute-start | bytes 3538952 | tf_op jit(solution)/shard_map/ppermute | solution.py:21
  12.0 91.7 %copy-start.8 = (f32[16]{0:T(128)S(1)}, f32[16]{0:T(128)}, u32[]{:S(2)}) copy-start(f32[16]{0:T(128)} %compare_convert_fusion) | copy-start | bytes 196
  12.0 0.6 copy-start.1
  101.9 1.7 copy-start.2
  103.7 286.6 %collective-permute-start.3 = (f32[3,16]{1,0:T(4,128)S(1)}, f32[3,16]{1,0:T(4,128)S(1)}, u32[]{:S(2)}, u32[]{:S(2)}) collective-permute-start(f32[3,16]{1,0:T(4,128)S(1)} %broadcast_multiply_fusion.2), channel_id=1, source_target_pairs={{0,4},{4,8},{8,12},{12,16},{16,20},{20,24},{24,28},{1,5},{5,9},{9,... | collective-permute-start | bytes 584 | tf_op jit(solution)/shard_map/ppermute | solution.py:21
  116.6 88.7 %copy-start.9 = (f32[16]{0:T(128)S(1)}, f32[16]{0:T(128)}, u32[]{:S(2)}) copy-start(f32[16]{0:T(128)} %compare_convert_fusion.1) | copy-start | bytes 196
  116.6 272.6 %copy-start.11 = (s32[16]{0:T(128)S(1)}, s32[16]{0:T(128)}, u32[]{:S(2)}) copy-start(s32[16]{0:T(128)} %and_select_fusion) | copy-start | bytes 196
  116.6 277.2 %copy-start.4 = (s32[705]{0:T(1024)S(1)}, s32[705]{0:T(1024)}, u32[]{:S(2)}) copy-start(s32[705]{0:T(1024)} %get-tuple-element.428) | copy-start | bytes 8464
  116.6 277.1 %copy-start.5 = (s32[705]{0:T(1024)S(1)}, s32[705]{0:T(1024)}, u32[]{:S(2)}) copy-start(s32[705]{0:T(1024)} %get-tuple-element.429) | copy-start | bytes 8464
  116.6 277.1 %copy-start.6 = (f32[705]{0:T(1024)S(1)}, f32[705]{0:T(1024)}, u32[]{:S(2)}) copy-start(f32[705]{0:T(1024)} %reduce.44) | copy-start | bytes 8464
  205.3 185.3 %collective-permute-start.2 = (f32[3,16]{1,0:T(4,128)S(1)}, f32[3,16]{1,0:T(4,128)S(1)}, u32[]{:S(2)}, u32[]{:S(2)}) collective-permute-start(f32[3,16]{1,0:T(4,128)S(1)} %broadcast_multiply_fusion.3), channel_id=1, source_target_pairs={{0,1},{1,2},{2,3},{4,5},{5,6},{6,7},{8,9},{9,10},{10,11},{12,13},{... | collective-permute-start | bytes 584 | tf_op jit(solution)/shard_map/ppermute | solution.py:21
  392.1 3.3 collective-permute-start.5
  395.5 4.2 collective-permute-start.4
  400.4 185.8 %collective-permute-start.6 = (f32[2,18,1]{1,0,2:T(2,128)S(1)}, f32[2,18,1]{1,0,2:T(2,128)S(1)}, u32[]{:S(2)}, u32[]{:S(2)}) collective-permute-start(f32[2,18,1]{1,0,2:T(2,128)S(1)} %get-tuple-element.515), channel_id=1, source_target_pairs={{1,0},{2,1},{3,2},{5,4},{6,5},{7,6},{9,8},{10,9},{11,10},{13,12},{... | collective-permute-start | bytes 440 | tf_op jit(solution)/shard_map/ppermute | solution.py:32
  401.7 185.8 %collective-permute-start.7 = (f32[2,18,1]{1,0,2:T(2,128)S(1)}, f32[2,18,1]{1,0,2:T(2,128)S(1)}, u32[]{:S(2)}, u32[]{:S(2)}) collective-permute-start(f32[2,18,1]{1,0,2:T(2,128)S(1)} %get-tuple-element.514), channel_id=1, source_target_pairs={{0,1},{1,2},{2,3},{4,5},{5,6},{6,7},{8,9},{9,10},{10,11},{12,13},{... | collective-permute-start | bytes 440 | tf_op jit(solution)/shard_map/ppermute | solution.py:29
  619.3 4.0 collective-permute-start.8
  623.6 3.1 collective-permute-start.9
  627.5 5.9 collective-permute-start.10
  628.8 5.8 collective-permute-start.11
  666.4 3.7 collective-permute-start.12
  670.4 3.1 collective-permute-start.13
  674.2 5.9 collective-permute-start.14
  675.5 5.8 collective-permute-start.15
